TPU v7x, 256 devices: a whole 4x4x8 slice. The times are simulated.
256 devices in a mesh: feeder: 64 (over z, x, core), node: 4 (over y).
Axes of the slice: x: 4, y: 4, z: 8, core: 2. Of those that a mesh axis runs over, the one named last changes fastest.
Arguments:
- factors: bfloat16 [2048, 256], P('node'), may hold values from -6 to 6
- loadings: bfloat16 [32768, 256], P(('feeder', 'node')), may hold values from -0.35355339 to 0.5
- parents: int32 [32768], P(('feeder', 'node')), may hold values from -1 to 126, as said below
- load_base: float32 [2, 32768], P(None, ('feeder', 'node')), may hold values from 2.4414063e-06 to 0.00048828125, as said below
- lateral_z: float32 [2, 32768], P(None, ('feeder', 'node')), may hold values from 0.007 to 0.175, as said below
- trunk_z: float32 [2, 64, 4], P(None, 'feeder', 'node'), may hold values from 0.00034375 to 0.00609375, as said below
Outputs:
- volt_real: float32 [2048, 32768], P(None, ('feeder', 'node'))
- volt_imag: float32 [2048, 32768], P(None, ('feeder', 'node'))
Inputs may be any that keep to these rules, and one draw needn't show every extreme that they name: `parents`: within each aligned run of 128 nodes (one lateral), a node's entry is the position of its parent in the same lateral, which comes before it, or -1 for a branch from the section's head node; the first node of every lateral has -1 and the last node's parent is the node just before it. `load_base`: with unit = 1 / 8192, row 0 lies between 1 and 4 units and row 1 between 0.02 and 0.08 units. `lateral_z`: with unit = 128 * 64 / 128^2, row 0 lies between 0.014 and 0.056 units and row 1 between 0.087 and 0.35 units. `trunk_z`: with unit = 1 / 64, row 0 lies between 0.022 and 0.066 units and row 1 between 0.13 and 0.39 units.
All inputs are finite; a program needn't handle non-finite values.
Results may differ from a plain program's by a relative error of at most 0.0003.
Values may be sent and summed in bfloat16 or wider, within the bound.
A program may use at most 64 MiB of HBM per device.

v0:
```python
import jax
import jax.numpy as jnp
from jax import lax
from jax.sharding import PartitionSpec as P

LAT_NODES = 128
SWEEPS = 3
HIGHEST = lax.Precision.HIGHEST


def carried_in(part, axis, combine, identity, reverse):
    count = lax.axis_size(axis)
    place = lax.axis_index(axis)
    ahead = count - 1 - place if reverse else place
    gathered = lax.all_gather(part, axis)
    state = jnp.zeros_like(part) + jnp.asarray(identity, part.dtype)

    def one(turn, state):
        source = count - 1 - turn if reverse else turn
        return combine(state, lax.dynamic_index_in_dim(gathered, source, 0, False))

    return lax.fori_loop(0, ahead, one, state)


def path_matrix(parent_rows):
    laterals, width = parent_rows.shape
    column = jnp.arange(width, dtype=jnp.int32)
    adjacency = (parent_rows[:, :, None] == column[None, None, :]).astype(jnp.float32)
    identity = jnp.eye(width, dtype=jnp.float32)
    paths = identity[None] + adjacency
    power = adjacency
    for turn in range((width - 1).bit_length() - 1):
        power = jnp.einsum("alm,amn->aln", power, power, precision=HIGHEST)
        paths = paths + jnp.einsum("alm,amn->aln", paths, power, precision=HIGHEST)
    return paths


def node_currents(active, reactive, real_part, imag_part):
    magnitude = real_part * real_part + imag_part * imag_part
    return (
        (active * real_part + reactive * imag_part) / magnitude,
        (active * imag_part - reactive * real_part) / magnitude,
    )


def add_total(earlier, later):
    return earlier + later


def lateral_products(stacked, tables):
    blocks = jnp.dot(stacked, tables[0], precision=HIGHEST, preferred_element_type=jnp.float32)
    return blocks


def trunk_heads(inject, trunk_z, scen):
    resist_trunk = trunk_z[0, 0, 0]
    react_trunk = trunk_z[1, 0, 0]
    zeros = jnp.zeros_like(inject)
    beyond = carried_in(inject, "feeder", add_total, zeros, True)
    trunk = inject + beyond
    trunk_real = trunk[:scen]
    trunk_imag = trunk[scen:]
    drop = jnp.concatenate(
        [
            resist_trunk * trunk_real - react_trunk * trunk_imag,
            resist_trunk * trunk_imag + react_trunk * trunk_real,
        ]
    )
    before = carried_in(drop, "feeder", add_total, zeros, False)
    total = before + drop
    return (1.0 - total[:scen], -total[scen:])


def local(factors, loadings, parents, load_base, lateral_z, trunk_z):
    levels = jnp.einsum(
        "sr,nr->sn",
        lax.all_gather(factors, "node", axis=0, tiled=True),
        loadings,
        preferred_element_type=jnp.float32,
    ).astype(jnp.bfloat16)
    scen = levels.shape[0]
    nodes_here = levels.shape[1]
    lat_count = nodes_here // LAT_NODES
    swing = 1.0 + 0.5 * jnp.tanh(levels.astype(jnp.float32))
    active = load_base[0][None, :] * swing
    reactive = load_base[1][None, :] * swing
    paths = path_matrix(parents.reshape(lat_count, LAT_NODES))
    paths_back = jnp.swapaxes(paths, 1, 2)
    resist = lateral_z[0][None, :]
    react = lateral_z[1][None, :]
    volts = jnp.concatenate(
        [jnp.ones((scen, nodes_here), jnp.float32), jnp.zeros((scen, nodes_here), jnp.float32)]
    )
    for sweep_index in range(SWEEPS):
        current_real, current_imag = node_currents(active, reactive, volts[:scen], volts[scen:])
        current = jnp.concatenate([current_real, current_imag])
        inject = jnp.sum(current, axis=1)
        branch = lateral_products(current, paths)
        branch_real = branch[:scen]
        branch_imag = branch[scen:]
        weighted = jnp.concatenate(
            [resist * branch_real - react * branch_imag, resist * branch_imag + react * branch_real]
        )
        drops = lateral_products(weighted, paths_back)
        head_real, head_imag = trunk_heads(inject, trunk_z, scen)
        volts = jnp.concatenate(
            [head_real[:, None] - drops[:scen], head_imag[:, None] - drops[scen:]]
        )
    return (volts[:scen], volts[scen:])


def solution(mesh):
    return jax.shard_map(
        local,
        mesh=mesh,
        in_specs=(
            P("node", None),
            P(("feeder", "node"), None),
            P(("feeder", "node")),
            P(None, ("feeder", "node")),
            P(None, ("feeder", "node")),
            P(None, "feeder", "node"),
        ),
        out_specs=(P(None, ("feeder", "node")), P(None, ("feeder", "node"))),
        check_vma=False,
    )
```

profile of v0, /device:TPU:1, one launch (start us, length us, event | category | flops | bytes accessed | tf_op | source)
XLA Modules:
  0.0 646.7 jit_solution(12022927235953794426)
XLA Ops:
  8.7 29.5 %all-gather.14.cloned.1.call-done = bf16[2048,256]{1,0:T(8,128)(2,1)} async-done(((bf16[512,256]{1,0:T(8,128)(2,1)}), bf16[2048,256]{1,0:T(8,128)(2,1)}) %all-gather.14.cloned.1.call-update) | async-done | bytes 1048592 | tf_op jit(solution)/shard_map/all_gather | solution.py:77
  38.2 1.7 multiply_add_fusion.5
  40.0 1.2 fusion.21
  43.6 77.6 %all-gather.16.cloned.1.call-done = f32[262144]{0:T(1024)} async-done(((f32[4096]{0:T(1024)}), f32[262144]{0:T(1024)}) %all-gather.16.cloned.1.call-update) | async-done | bytes 1048592 | tf_op jit(solution)/shard_map/all_gather | solution.py:15
  121.2 2.4 reshape.172
  123.6 59.7 %while.66 = (s32[]{:T(128)}, f32[4096]{0:T(1024)S(1)}, s32[]{:T(128)}, f32[64,4096]{1,0:T(8,128)}, s32[]{:T(128)}, /*index=5*/s32[]{:T(128)}, s32[]{:T(128)}, s32[]{:T(128)}) while((s32[]{:T(128)}, f32[4096]{0:T(1024)S(1)}, s32[]{:T(128)}, f32[64,4096]{1,0:T(8,128)}, s32[]{:T(128)}, /*index=5*/s32[]{:T(128)}, s32[]{:T(128)}, s32[]{:T(128)}) %tuple.128), condition=%wide.region_2.3_spmd, body=%wide.region_1.2_spmd.sunk | while | flops 4102 | bytes 82055 | solution.py:22
  126.4 0.9 constant_dynamic-slice_fusion.12
  127.4 0.9 constant_dynamic-slice_fusion.12
  128.4 0.9 constant_dynamic-slice_fusion.12
  129.3 0.9 constant_dynamic-slice_fusion.12
  130.3 0.9 constant_dynamic-slice_fusion.12
  135.1 0.9 constant_dynamic-slice_fusion.12
  136.1 0.9 constant_dynamic-slice_fusion.12
  137.0 0.9 constant_dynamic-slice_fusion.12
  138.0 0.9 constant_dynamic-slice_fusion.12
  139.0 0.9 constant_dynamic-slice_fusion.12
  139.9 0.9 constant_dynamic-slice_fusion.12
  144.7 0.9 constant_dynamic-slice_fusion.12
  145.7 0.9 constant_dynamic-slice_fusion.12
  146.7 0.9 constant_dynamic-slice_fusion.12
  147.6 0.9 constant_dynamic-slice_fusion.12
  148.6 0.9 constant_dynamic-slice_fusion.12
  153.4 0.9 constant_dynamic-slice_fusion.12
  154.4 0.9 constant_dynamic-slice_fusion.12
  155.3 0.9 constant_dynamic-slice_fusion.12
  156.3 0.9 constant_dynamic-slice_fusion.12
  157.3 0.9 constant_dynamic-slice_fusion.12
  158.2 0.9 constant_dynamic-slice_fusion.12
  163.0 0.9 constant_dynamic-slice_fusion.12
  164.0 0.9 constant_dynamic-slice_fusion.12
  165.0 0.9 constant_dynamic-slice_fusion.12
  165.9 0.9 constant_dynamic-slice_fusion.12
  166.9 0.9 constant_dynamic-slice_fusion.12
  171.7 0.9 constant_dynamic-slice_fusion.12
  172.7 0.9 constant_dynamic-slice_fusion.12
  173.6 0.9 constant_dynamic-slice_fusion.12
  174.6 0.9 constant_dynamic-slice_fusion.12
  175.6 0.9 constant_dynamic-slice_fusion.12
  183.3 1.2 multiply_subtract_fusion.6
  186.0 1.9 fusion.20
  188.2 3.2 fusion.4
  191.3 65.4 %all-gather.18.cloned.1.call-done = f32[262144]{0:T(1024)} async-done(((f32[4096]{0:T(1024)}), f32[262144]{0:T(1024)}) %all-gather.18.cloned.1.call-update) | async-done | bytes 1048592 | tf_op jit(solution)/shard_map/all_gather | solution.py:15
  256.7 1.4 reshape.173
  258.2 2.0 fusion.23
  260.2 1.2 fusion.19
  261.5 77.3 %all-gather.20.cloned.1.call-done = f32[262144]{0:T(1024)} async-done(((f32[4096]{0:T(1024)}), f32[262144]{0:T(1024)}) %all-gather.20.cloned.1.call-update) | async-done | bytes 1048592 | tf_op jit(solution)/shard_map/all_gather | solution.py:15
  338.8 2.4 reshape.174
  341.2 59.7 %while.68 = (s32[]{:T(128)}, f32[4096]{0:T(1024)S(1)}, s32[]{:T(128)}, f32[64,4096]{1,0:T(8,128)}, s32[]{:T(128)}, /*index=5*/s32[]{:T(128)}, s32[]{:T(128)}, s32[]{:T(128)}) while((s32[]{:T(128)}, f32[4096]{0:T(1024)S(1)}, s32[]{:T(128)}, f32[64,4096]{1,0:T(8,128)}, s32[]{:T(128)}, /*index=5*/s32[]{:T(128)}, s32[]{:T(128)}, s32[]{:T(128)}) %tuple.134), condition=%wide.region_7.8_spmd, body=%wide.region_6.7_spmd.sunk | while | flops 4102 | bytes 82055 | solution.py:22
  400.9 1.2 multiply_subtract_fusion.5
  403.0 1.9 fusion.18
  405.1 3.2 fusion.8
  408.3 66.1 %all-gather.22.cloned.1.call-done = f32[262144]{0:T(1024)} async-done(((f32[4096]{0:T(1024)}), f32[262144]{0:T(1024)}) %all-gather.22.cloned.1.call-update) | async-done | bytes 1048592 | tf_op jit(solution)/shard_map/all_gather | solution.py:15
  474.3 1.4 reshape.175
  475.9 2.0 fusion.22
  477.9 1.2 fusion.17
  479.2 77.3 %all-gather.24.cloned.1.call-done = f32[262144]{0:T(1024)} async-done(((f32[4096]{0:T(1024)}), f32[262144]{0:T(1024)}) %all-gather.24.cloned.1.call-update) | async-done | bytes 1048592 | tf_op jit(solution)/shard_map/all_gather | solution.py:15
  556.5 1.4 reshape.176
  557.9 4.0 while.70
  562.0 1.2 multiply_subtract_fusion.4
  563.8 1.9 fusion.16
  565.9 1.8 fusion.12
  567.7 68.9 %all-gather.26.cloned.1.call-done = f32[262144]{0:T(1024)} async-done(((f32[4096]{0:T(1024)}), f32[262144]{0:T(1024)}) %all-gather.26.cloned.1.call-update) | async-done | bytes 1048592 | tf_op jit(solution)/shard_map/all_gather | solution.py:15
  636.6 1.4 reshape.177
  638.2 1.7 slice_subtract_fusion
  (413 shorter events, 95.1 us)
Async XLA Ops:
  7.2 31.1 %copy-start = (bf16[128,256]{1,0:T(8,128)(2,1)S(1)}, bf16[128,256]{1,0:T(8,128)(2,1)}, u32[]{:S(2)}) copy-start(bf16[128,256]{1,0:T(8,128)(2,1)} %param.19) | copy-start | bytes 196612
  7.2 31.0 %all-gather.14.cloned.1.call-start = ((), (), s32[]{:S(2)}) async-start(), calls=%async_computation | async-start | bytes 1310720 | tf_op jit(solution)/shard_map/all_gather | solution.py:77
  7.9 113.3 %all-gather.16.cloned.1.call-start = ((), (), s32[]{:S(2)}) async-start(), calls=%async_computation.1 | async-start | bytes 1064960 | tf_op jit(solution)/shard_map/all_gather | solution.py:15
  40.0 1.3 copy-start.5
  40.0 1.9 copy-start.4
  41.2 142.0 %copy-start.1 = (f32[4096]{0:T(1024)S(1)}, f32[4096]{0:T(1024)}, u32[]{:S(2)}) copy-start(f32[4096]{0:T(1024)} %fusion.21) | copy-start | bytes 49156
  41.2 215.4 %all-gather.18.cloned.1.call-start = ((), (), s32[]{:S(2)}) async-start(), calls=%async_computation.2 | async-start | bytes 1064960 | tf_op jit(solution)/shard_map/all_gather | solution.py:15
  42.1 143.1 %copy-start.6 = (f32[2,128]{1,0:T(2,128)S(1)}, f32[2,128]{1,0:T(2,128)}, u32[]{:S(2)}) copy-start(f32[2,128]{1,0:T(2,128)} %param.22) | copy-start | bytes 3076
  185.1 153.7 %all-gather.20.cloned.1.call-start = ((), (), s32[]{:S(2)}) async-start(), calls=%async_computation.3 | async-start | bytes 1064960 | tf_op jit(solution)/shard_map/all_gather | solution.py:15
  261.4 139.5 %copy-start.3 = (f32[4096]{0:T(1024)S(1)}, f32[4096]{0:T(1024)}, u32[]{:S(2)}) copy-start(f32[4096]{0:T(1024)} %fusion.19) | copy-start | bytes 49156
  261.4 212.9 %all-gather.22.cloned.1.call-start = ((), (), s32[]{:S(2)}) async-start(), calls=%async_computation.4 | async-start | bytes 1064960 | tf_op jit(solution)/shard_map/all_gather | solution.py:15
  402.8 153.7 %all-gather.24.cloned.1.call-start = ((), (), s32[]{:S(2)}) async-start(), calls=%async_computation.5 | async-start | bytes 1064960 | tf_op jit(solution)/shard_map/all_gather | solution.py:15
  479.1 82.9 %copy-start.2 = (f32[4096]{0:T(1024)S(1)}, f32[4096]{0:T(1024)}, u32[]{:S(2)}) copy-start(f32[4096]{0:T(1024)} %fusion.17) | copy-start | bytes 49156
  479.1 157.5 %all-gather.26.cloned.1.call-start = ((), (), s32[]{:S(2)}) async-start(), calls=%async_computation.6 | async-start | bytes 1064960 | tf_op jit(solution)/shard_map/all_gather | solution.py:15
Sparse Core Ops, SparseCore 0:
  9.8 28.3 all-gather.13
  41.6 79.5 all-gather.15
  185.2 71.4 all-gather.17
  261.6 77.2 all-gather.19
  402.9 71.4 all-gather.21
  479.2 77.2 all-gather.23
  563.9 72.6 all-gather.25
where the time goes:
time: 649 us; the launch traced here: 647 us
  waiting for transfers between devices  463 us (71%)
  local copies, waits for them, and re-layouts  127 us (20%)
  matrix products  18 us (3%)
  other arithmetic  16.4 us (3%)
  between operations  14.6 us (2%)
  loops' own time  6.86 us (1%)
    all_gather x6, waiting for transfers between devices, carried_in(): gathered = lax.all_gather(part, axis)  433 us
    dynamic_slice x189, local copies, waits for them, and re-layouts, one(): return combine(state, lax.dynamic_index_in_dim(gathered, source, 0, False))  116 us
    all_gather x1, waiting for transfers between devices, local(): lax.all_gather(factors, 'node', axis=0, tiled=True)  29.5 us
    dot_general x6, matrix products, lateral_products(): jnp.dot(stacked, tables[0], precision=HIGHEST, preferred_element_type=jnp...  13.8 us
  transfers between devices with their start and end apart: 7, of which 7 were waited for; matrix products, arithmetic and copies ran while one was open for 3% of the time, Pallas kernels for 0%

commit v1 on v0

--- a/solution.py
+++ b/solution.py
@@ -74,7 +74,9 @@
 def local(factors, loadings, parents, load_base, lateral_z, trunk_z):
     levels = jnp.einsum(
         "sr,nr->sn",
-        lax.all_gather(factors, "node", axis=0, tiled=True),
+        jnp.concatenate(
+            lax.all_to_all(jnp.stack([factors] * lax.axis_size("node")), "node", 0, 0), axis=0
+        ),
         loadings,
         preferred_element_type=jnp.float32,
     ).astype(jnp.bfloat16)

time: 649 us -> 697 us (1.074)
  local copies, waits for them, and re-layouts: 127 us -> 187 us
  waiting for transfers between devices: 463 us -> 445 us
    dynamic_slice x189, local copies, waits for them, and re-layouts: 116 us -> 172 us  [one(): return combine(state, lax.dynamic_index_in_dim(gathered, source, 0, False))]
    all_gather x1 -> x0, waiting for transfers between devices: 29.5 us -> none  [local(): lax.all_gather(factors, 'node', axis=0, tiled=True)]
    all_to_all x0 -> x1, waiting for transfers between devices: none -> 13.5 us  [local(): lax.all_to_all(jnp.stack([factors] * lax.axis_size('node')), 'node', 0, 0)]
where the time goes in v1:
time: 697 us; the launch traced here: 693 us
  waiting for transfers between devices  445 us (64%)
  local copies, waits for them, and re-layouts  187 us (27%)
  matrix products  18.1 us (3%)
  other arithmetic  16.4 us (2%)
  between operations  14.5 us (2%)
    all_gather x6, waiting for transfers between devices, carried_in(): gathered = lax.all_gather(part, axis)  432 us
    dynamic_slice x189, local copies, waits for them, and re-layouts, one(): return combine(state, lax.dynamic_index_in_dim(gathered, source, 0, False))  172 us
  transfers between devices with their start and end apart: 7, of which 7 were waited for; matrix products, arithmetic and copies ran while one was open for 3% of the time, Pallas kernels for 0%

profile of v1, /device:TPU:1, one launch (start us, length us, event | category | flops | bytes accessed | tf_op | source)
XLA Modules:
  0.0 692.8 jit_solution(8504464732582287394)
XLA Ops:
  7.2 2.0 stack.2
  9.2 5.0 all-to-all-start
  14.2 13.5 %all-to-all-done = bf16[4,512,256]{2,1,0:T(8,128)(2,1)S(1)} async-done(((bf16[4,512,256]{2,1,0:T(8,128)(2,1)}), bf16[4,512,256]{2,1,0:T(8,128)(2,1)S(1)}, u32[]{:S(2)}, u32[]{:S(2)}) %all-to-all-start) | async-done | bytes 1048608 | tf_op jit(solution)/shard_map/all_to_all | solution.py:78
  27.7 1.0 copy-done.1
  28.7 1.7 multiply_add_fusion.5
  30.5 1.2 fusion.21
  34.1 77.8 %all-gather.13.cloned.1.call-done = f32[262144]{0:T(1024)} async-done(((f32[4096]{0:T(1024)}), f32[262144]{0:T(1024)}) %all-gather.13.cloned.1.call-update) | async-done | bytes 1048592 | tf_op jit(solution)/shard_map/all_gather | solution.py:15
  111.9 2.4 reshape.178
  114.3 59.7 %while.66 = (s32[]{:T(128)}, f32[4096]{0:T(1024)S(1)}, s32[]{:T(128)}, f32[64,4096]{1,0:T(8,128)}, s32[]{:T(128)}, /*index=5*/s32[]{:T(128)}, s32[]{:T(128)}, s32[]{:T(128)}) while((s32[]{:T(128)}, f32[4096]{0:T(1024)S(1)}, s32[]{:T(128)}, f32[64,4096]{1,0:T(8,128)}, s32[]{:T(128)}, /*index=5*/s32[]{:T(128)}, s32[]{:T(128)}, s32[]{:T(128)}) %tuple.128), condition=%wide.region_2.3_spmd, body=%wide.region_1.2_spmd.sunk | while | flops 4102 | bytes 82055 | solution.py:22
  115.2 0.9 constant_dynamic-slice_fusion.12
  120.1 0.9 constant_dynamic-slice_fusion.12
  121.0 0.9 constant_dynamic-slice_fusion.12
  122.0 0.9 constant_dynamic-slice_fusion.12
  122.9 0.9 constant_dynamic-slice_fusion.12
  123.9 0.9 constant_dynamic-slice_fusion.12
  124.9 0.9 constant_dynamic-slice_fusion.12
  129.7 0.9 constant_dynamic-slice_fusion.12
  130.7 0.9 constant_dynamic-slice_fusion.12
  131.6 0.9 constant_dynamic-slice_fusion.12
  132.6 0.9 constant_dynamic-slice_fusion.12
  133.5 0.9 constant_dynamic-slice_fusion.12
  138.4 0.9 constant_dynamic-slice_fusion.12
  139.3 0.9 constant_dynamic-slice_fusion.12
  140.3 0.9 constant_dynamic-slice_fusion.12
  141.2 0.9 constant_dynamic-slice_fusion.12
  142.2 0.9 constant_dynamic-slice_fusion.12
  143.2 0.9 constant_dynamic-slice_fusion.12
  148.0 0.9 constant_dynamic-slice_fusion.12
  148.9 0.9 constant_dynamic-slice_fusion.12
  149.9 0.9 constant_dynamic-slice_fusion.12
  150.9 0.9 constant_dynamic-slice_fusion.12
  151.8 0.9 constant_dynamic-slice_fusion.12
  156.7 0.9 constant_dynamic-slice_fusion.12
  157.6 0.9 constant_dynamic-slice_fusion.12
  158.6 0.9 constant_dynamic-slice_fusion.12
  159.5 0.9 constant_dynamic-slice_fusion.12
  160.5 0.9 constant_dynamic-slice_fusion.12
  161.5 0.9 constant_dynamic-slice_fusion.12
  174.0 1.2 multiply_subtract_fusion.6
  176.7 1.9 fusion.20
  178.9 3.2 fusion.4
  182.0 65.4 %all-gather.15.cloned.1.call-done = f32[262144]{0:T(1024)} async-done(((f32[4096]{0:T(1024)}), f32[262144]{0:T(1024)}) %all-gather.15.cloned.1.call-update) | async-done | bytes 1048592 | tf_op jit(solution)/shard_map/all_gather | solution.py:15
  247.4 1.4 reshape.179
  248.9 2.0 fusion.23
  250.9 1.2 fusion.19
  252.2 77.3 %all-gather.17.cloned.1.call-done = f32[262144]{0:T(1024)} async-done(((f32[4096]{0:T(1024)}), f32[262144]{0:T(1024)}) %all-gather.17.cloned.1.call-update) | async-done | bytes 1048592 | tf_op jit(solution)/shard_map/all_gather | solution.py:15
  329.6 2.4 reshape.180
  331.9 59.7 %while.68 = (s32[]{:T(128)}, f32[4096]{0:T(1024)S(1)}, s32[]{:T(128)}, f32[64,4096]{1,0:T(8,128)}, s32[]{:T(128)}, /*index=5*/s32[]{:T(128)}, s32[]{:T(128)}, s32[]{:T(128)}) while((s32[]{:T(128)}, f32[4096]{0:T(1024)S(1)}, s32[]{:T(128)}, f32[64,4096]{1,0:T(8,128)}, s32[]{:T(128)}, /*index=5*/s32[]{:T(128)}, s32[]{:T(128)}, s32[]{:T(128)}) %tuple.134), condition=%wide.region_7.8_spmd, body=%wide.region_6.7_spmd.sunk | while | flops 4102 | bytes 82055 | solution.py:22
  391.7 1.2 multiply_subtract_fusion.5
  393.7 1.9 fusion.18
  395.8 3.2 fusion.8
  399.0 66.1 %all-gather.19.cloned.1.call-done = f32[262144]{0:T(1024)} async-done(((f32[4096]{0:T(1024)}), f32[262144]{0:T(1024)}) %all-gather.19.cloned.1.call-update) | async-done | bytes 1048592 | tf_op jit(solution)/shard_map/all_gather | solution.py:15
  465.1 1.4 reshape.181
  466.6 2.0 fusion.22
  468.6 1.2 fusion.17
  469.9 77.3 %all-gather.21.cloned.1.call-done = f32[262144]{0:T(1024)} async-done(((f32[4096]{0:T(1024)}), f32[262144]{0:T(1024)}) %all-gather.21.cloned.1.call-update) | async-done | bytes 1048592 | tf_op jit(solution)/shard_map/all_gather | solution.py:15
  547.2 2.4 reshape.182
  549.6 59.7 %while.70 = (s32[]{:T(128)}, f32[4096]{0:T(1024)S(1)}, s32[]{:T(128)}, f32[64,4096]{1,0:T(8,128)}, s32[]{:T(128)}, /*index=5*/s32[]{:T(128)}, s32[]{:T(128)}, s32[]{:T(128)}) while((s32[]{:T(128)}, f32[4096]{0:T(1024)S(1)}, s32[]{:T(128)}, f32[64,4096]{1,0:T(8,128)}, s32[]{:T(128)}, /*index=5*/s32[]{:T(128)}, s32[]{:T(128)}, ...), condition=%wide.region_12.13_spmd, body=%wide.region_11.12_spmd.sunk | while | flops 4102 | bytes 82055 | solution.py:22
  609.3 1.2 multiply_subtract_fusion.4
  611.1 1.9 fusion.16
  613.3 1.8 fusion.12
  615.1 67.6 %all-gather.23.cloned.1.call-done = f32[262144]{0:T(1024)} async-done(((f32[4096]{0:T(1024)}), f32[262144]{0:T(1024)}) %all-gather.23.cloned.1.call-update) | async-done | bytes 1048592 | tf_op jit(solution)/shard_map/all_gather | solution.py:15
  682.7 1.4 reshape.183
  684.3 1.7 slice_subtract_fusion
  (417 shorter events, 152.3 us)
Async XLA Ops:
  7.2 21.5 %copy-start = (bf16[128,256]{1,0:T(8,128)(2,1)S(1)}, bf16[128,256]{1,0:T(8,128)(2,1)}, u32[]{:S(2)}) copy-start(bf16[128,256]{1,0:T(8,128)(2,1)} %param.19) | copy-start | bytes 196612
  7.2 7.0 %copy-start.7 = (f32[2,128]{1,0:T(2,128)S(1)}, f32[2,128]{1,0:T(2,128)}, u32[]{:S(2)}) copy-start(f32[2,128]{1,0:T(2,128)} %param.21) | copy-start | bytes 3076
  9.2 18.5 %all-to-all-start = ((bf16[4,512,256]{2,1,0:T(8,128)(2,1)}), bf16[4,512,256]{2,1,0:T(8,128)(2,1)S(1)}, u32[]{:S(2)}, u32[]{:S(2)}) async-start(bf16[4,512,256]{2,1,0:T(8,128)(2,1)} %stack.2), calls=%async_computation | async-start | bytes 2097152 | tf_op jit(solution)/shard_map/all_to_all | solution.py:78
  14.2 97.7 %all-gather.13.cloned.1.call-start = ((), (), s32[]{:S(2)}) async-start(), calls=%async_computation.1 | async-start | bytes 1064960 | tf_op jit(solution)/shard_map/all_gather | solution.py:15
  27.7 1.0 copy-start.1
  30.4 1.3 copy-start.6
  30.5 1.9 copy-start.5
  31.7 142.3 %copy-start.2 = (f32[4096]{0:T(1024)S(1)}, f32[4096]{0:T(1024)}, u32[]{:S(2)}) copy-start(f32[4096]{0:T(1024)} %fusion.21) | copy-start | bytes 49156
  31.7 215.7 %all-gather.15.cloned.1.call-start = ((), (), s32[]{:S(2)}) async-start(), calls=%async_computation.2 | async-start | bytes 1064960 | tf_op jit(solution)/shard_map/all_gather | solution.py:15
  32.6 143.3 %copy-start.8 = (f32[2,128]{1,0:T(2,128)S(1)}, f32[2,128]{1,0:T(2,128)}, u32[]{:S(2)}) copy-start(f32[2,128]{1,0:T(2,128)} %param.22) | copy-start | bytes 3076
  175.8 153.7 %all-gather.17.cloned.1.call-start = ((), (), s32[]{:S(2)}) async-start(), calls=%async_computation.3 | async-start | bytes 1064960 | tf_op jit(solution)/shard_map/all_gather | solution.py:15
  252.1 139.5 %copy-start.4 = (f32[4096]{0:T(1024)S(1)}, f32[4096]{0:T(1024)}, u32[]{:S(2)}) copy-start(f32[4096]{0:T(1024)} %fusion.19) | copy-start | bytes 49156
  252.2 212.9 %all-gather.19.cloned.1.call-start = ((), (), s32[]{:S(2)}) async-start(), calls=%async_computation.4 | async-start | bytes 1064960 | tf_op jit(solution)/shard_map/all_gather | solution.py:15
  393.5 153.7 %all-gather.21.cloned.1.call-start = ((), (), s32[]{:S(2)}) async-start(), calls=%async_computation.5 | async-start | bytes 1064960 | tf_op jit(solution)/shard_map/all_gather | solution.py:15
  469.8 139.5 %copy-start.3 = (f32[4096]{0:T(1024)S(1)}, f32[4096]{0:T(1024)}, u32[]{:S(2)}) copy-start(f32[4096]{0:T(1024)} %fusion.17) | copy-start | bytes 49156
  469.8 212.9 %all-gather.23.cloned.1.call-start = ((), (), s32[]{:S(2)}) async-start(), calls=%async_computation.6 | async-start | bytes 1064960 | tf_op jit(solution)/shard_map/all_gather | solution.py:15
Sparse Core Ops, SparseCore 0:
  31.8 80.0 all-gather.12
  175.9 71.4 all-gather.14
  252.3 77.2 all-gather.16
  393.6 71.4 all-gather.18
  469.9 77.2 all-gather.20
  611.3 71.4 all-gather.22
